TPU v7x, 32 devices: a whole 2x2x4 slice. The times are simulated.
32 devices in a mesh: grp: 2 (over y), head: 4 (over z), tm: 4 (over x, core).
Axes of the slice: x: 2, y: 2, z: 4, core: 2. Of those that a mesh axis runs over, the one named last changes fastest.
Arguments:
- query_rows: bfloat16 [32, 64, 3072], P(('grp', 'tm'), 'head'), parts along dimension 0, may hold values from -180 to 180
- key_rows: bfloat16 [32, 64, 3072], P(('grp', 'tm'), 'head'), parts along dimension 0, may hold values from -6 to 6
- value_rows: bfloat16 [32, 64, 3072], P(('grp', 'tm'), 'head'), parts along dimension 0, may hold values from -6 to 6
- pair_list: int32 [32, 32], P('grp'), parts along dimension 0, may hold values from 0 to 15, as said below
- block_tokens: int32 [32], P('grp'), parts along dimension 0, may hold values from 1 to 64, 768 in all
Outputs:
- attended: bfloat16 [32, 64, 3072], P(('grp', 'tm'), 'head'), parts along dimension 0
There are 2 independent parts, one for each index of `grp`. A program takes and returns all parts, laid end to end along the dimension named above; each array names one. Nothing has to cross between parts.
Inputs may be any that keep to these rules, and one draw needn't show every extreme that they name: `pair_list`: row q names q in column 0 and q xor 1 in column 1; a block may be named twice in a row. The query blocks of one time shard name at most 2 different blocks of a time shard beside it and at most 1 of a time shard two or more away; both bounds are reached.
All inputs are finite; a program needn't handle non-finite values.
Results may differ from a plain program's by a relative error of at most 0.0012.
The roundings to bfloat16 on the way count: a program that leaves them out, or rounds other values in their place, can miss the bound.
Values may be sent and summed in bfloat16 or wider, within the bound.
A program may use at most 128 MiB of HBM per device.

v0:
```python
import functools
import math

import jax
import jax.numpy as jnp
from jax import lax
from jax.experimental import pallas as pl
from jax.experimental.pallas import tpu as pltpu
from jax.sharding import PartitionSpec as P

HD = 128
NEAR_CAP = 2
FAR_CAP = 1
LANES = 128
LEAD = 2
MESH = pl.DeviceIdType.MESH


def incoming_slots(count_tm):
    slots = []
    for offset in range(1, count_tm):
        capacity = NEAR_CAP if offset in (1, count_tm - 1) else FAR_CAP
        slots += [(offset, place) for place in range(capacity)]
    return slots


def partner(index, offset, count):
    if count & (count - 1):
        return lax.rem(index + offset, count)
    for level in range(count.bit_length() - 1):
        if offset >> level & 1:
            bit = lax.rem(lax.div(index, 1 << level), 2)
            index = index + (1 << level) * (1 - 2 * bit)
    return index


def sign_table(dimension):
    rows = lax.broadcasted_iota(jnp.int32, (dimension, dimension), 0)
    columns = lax.broadcasted_iota(jnp.int32, (dimension, dimension), 1)
    common = rows & columns
    parity = jnp.zeros((dimension, dimension), jnp.int32)
    for bit_level in range(dimension.bit_length() - 1):
        parity = parity + ((common >> bit_level) & 1)
    return jnp.where((parity & 1) == 0, 1.0, -1.0).astype(jnp.float32)


def kernel(
    sizes,
    query_ref,
    key_ref,
    value_ref,
    pair_ref,
    tokens_far,
    out_ref,
    gathered,
    store,
    outbox,
    staged,
    pair_here,
    tokens_ref,
    listed_ref,
    place_ref,
    wanted_ref,
    bias_ref,
    sign_ref,
    head_send,
    head_recv,
    local_sem,
    halo_send,
    halo_recv,
    back_send,
    back_recv,
    back_local,
    pair_sem,
    tokens_sem,
):
    count_head, count_tm, blocks, part, heads, block, total_blocks, slots, padded = sizes
    width = heads * HD
    my_head = lax.axis_index("head")
    me = lax.axis_index("tm")
    scale = 1.0 / math.sqrt(HD)
    slot_of = {slot: i for i, slot in enumerate(slots)}
    sources = (key_ref, value_ref, query_ref)

    for offset in reversed(range(1, count_head)):
        peer = partner(my_head, offset, count_head)
        pl.semaphore_signal(
            pltpu.get_barrier_semaphore(), inc=1, device_id={"head": peer}, device_id_type=MESH
        )

    def columns_of(owner, h):
        return pl.ds(pl.multiple_of(owner * width + h * HD, HD), HD)

    def head_copy(which, offset, h):
        peer = partner(my_head, offset, count_head)
        return pltpu.make_async_remote_copy(
            src_ref=sources[which].at[:, :, columns_of(peer, h)],
            dst_ref=gathered.at[which, h, my_head],
            send_sem=head_send.at[which, offset - 1, h],
            recv_sem=head_recv.at[which, offset - 1, h],
            device_id={"head": peer},
            device_id_type=MESH,
        )

    def local_copy(which, h):
        return pltpu.make_async_copy(
            sources[which].at[:, :, columns_of(my_head, h)],
            gathered.at[which, h, my_head],
            local_sem.at[which, h],
        )

    def halo_copy(which, h, slot):
        offset, place = slot
        peer = lax.rem(me + offset, count_tm)
        landing = slot_of[(count_tm - offset, place)]
        return pltpu.make_async_remote_copy(
            src_ref=outbox.at[which, h, slot_of[slot]],
            dst_ref=store.at[which, h, blocks + landing],
            send_sem=halo_send.at[which, h, slot_of[slot]],
            recv_sem=halo_recv.at[which, h, landing],
            device_id={"tm": peer},
            device_id_type=MESH,
        )

    def halo_arrival(which, h, slot):
        i = slot_of[slot]
        peer = lax.rem(me + slot[0], count_tm)
        return pltpu.make_async_remote_copy(
            src_ref=outbox.at[which, h, i],
            dst_ref=store.at[which, h, blocks + i],
            send_sem=halo_send.at[which, h, i],
            recv_sem=halo_recv.at[which, h, i],
            device_id={"tm": peer},
            device_id_type=MESH,
        )

    def if_used(slot, action):
        if slot[1] < FAR_CAP:
            action()
        else:
            peer = lax.rem(me + slot[0], count_tm)
            near = (peer == me + 1) | (peer == me - 1)
            pl.when(near)(action)

    def back_copy(offset, h):
        peer = partner(my_head, offset, count_head)
        return pltpu.make_async_remote_copy(
            src_ref=staged.at[h, peer],
            dst_ref=out_ref.at[:, :, columns_of(my_head, h)],
            send_sem=back_send.at[offset - 1, h],
            recv_sem=back_recv.at[offset - 1, h],
            device_id={"head": peer},
            device_id_type=MESH,
        )

    def back_own(h):
        return pltpu.make_async_copy(
            staged.at[h, my_head],
            out_ref.at[:, :, columns_of(my_head, h)],
            back_local.at[h],
        )

    store[:, :, blocks:] = jnp.zeros((2, heads, padded - blocks, block, HD), jnp.bfloat16)
    for offset in range(1, count_tm):
        peer = lax.rem(me + offset, count_tm)
        pl.semaphore_signal(
            pltpu.get_barrier_semaphore(), inc=1, device_id={"tm": peer}, device_id_type=MESH
        )
    pair_copy = pltpu.make_async_copy(pair_ref, pair_here, pair_sem)
    pair_copy.start()
    tokens_copy = pltpu.make_async_copy(tokens_far, tokens_ref, tokens_sem)
    tokens_copy.start()

    sign_ref[...] = sign_table(HD).astype(jnp.bfloat16)
    pl.semaphore_wait(pltpu.get_barrier_semaphore(), count_head - 1 + count_tm - 1)

    def start_remote(which, h):
        for offset in reversed(range(1, count_head)):
            head_copy(which, offset, h).start()

    def start_step(h, carry):
        @pl.when(h < heads)
        def _():
            start_remote(0, h)
            start_remote(1, h)

        pl.when(h >= LEAD)(lambda: start_remote(2, h - LEAD))
        return carry

    lax.fori_loop(0, heads + LEAD, start_step, 0)

    def start_local(h, carry):
        for which in range(3):
            local_copy(which, h).start()
        return carry

    lax.fori_loop(0, heads, start_local, 0)

    pair_copy.wait()
    tokens_copy.wait()
    pairs = pair_here[...]
    lane = lax.broadcasted_iota(jnp.int32, (1, LANES), 1)
    listed = jnp.zeros((total_blocks, LANES), jnp.float32)
    token_row = jnp.zeros((1, LANES), jnp.float32)
    for k in range(total_blocks):
        found = jnp.max(jnp.where(pairs == k, 1.0, 0.0), axis=1, keepdims=True)
        here = jnp.where(lane == k, 1.0, 0.0)
        listed = listed + found * here
        token_row = token_row + here * tokens_ref[k].astype(jnp.float32)
    wanted_ref[...] = jnp.zeros_like(wanted_ref)
    for t in range(count_tm):
        of_shard = listed[t * blocks : (t + 1) * blocks]
        listed_ref[t] = of_shard
        wanted_ref[t : t + 1, :] = jnp.max(of_shard, axis=0, keepdims=True)
    low = lax.broadcasted_iota(jnp.int32, (LANES, LANES), 0)
    high = lax.broadcasted_iota(jnp.int32, (LANES, LANES), 1)
    low_shard, high_shard = jnp.zeros_like(low), jnp.zeros_like(high)
    lane_shard = jnp.zeros_like(lane)
    for t in range(1, count_tm):
        low_shard = low_shard + jnp.where(low >= t * blocks, 1, 0)
        high_shard = high_shard + jnp.where(high >= t * blocks, 1, 0)
        lane_shard = lane_shard + jnp.where(lane >= t * blocks, 1, 0)
    before = jnp.where((low_shard == high_shard) & (low < high), 1.0, 0.0).astype(jnp.bfloat16)
    wanted = wanted_ref[...]
    rank = jnp.dot(wanted.astype(jnp.bfloat16), before, preferred_element_type=jnp.float32)
    for place in range(NEAR_CAP):
        chosen = jnp.where(rank == float(place), wanted, 0.0)
        for t in range(count_tm):
            place_ref[place, t] = chosen[t : t + 1, :]
    picks = []
    for offset, place in slots:
        row = place_ref[place, lax.rem(me + offset, count_tm)]
        picks.append(
            [
                jnp.sum(jnp.where(lane == me * blocks + j, row, 0.0), axis=1, keepdims=True)
                for j in range(blocks)
            ]
        )
    mine = listed_ref[me]
    key_lane = lax.broadcasted_iota(jnp.int32, (1, padded * block), 1)
    key_end = jnp.zeros((blocks, padded * block), jnp.float32)
    for i in range(blocks + len(slots)):
        if i < blocks:
            kept_tokens = jnp.where(lane == me * blocks + i, token_row, 0.0)
        else:
            offset, place = slots[i - blocks]
            owner = lax.rem(me + offset, count_tm)
            row = place_ref[place, me]
            kept_tokens = jnp.where(lane_shard == owner, row * token_row, 0.0)
        kept = jnp.sum(mine * kept_tokens, axis=1, keepdims=True)
        inside = jnp.where((key_lane >= i * block) & (key_lane < (i + 1) * block), 1.0, 0.0)
        key_end = key_end + inside * (kept + float(i * block))
    bias_ref[...] = jnp.where(key_lane.astype(jnp.float32) < key_end, 0.0, -1e30)

    def arrived(which, h):
        local_copy(which, h).wait()
        for offset in reversed(range(1, count_head)):
            head_copy(which, offset, h).wait_recv()
        rows = jnp.concatenate(
            [
                gathered[which, h, :, b].astype(jnp.float32).reshape(block, HD)
                for b in range(blocks)
            ],
            axis=0,
        ).astype(jnp.bfloat16)
        turned = jnp.dot(rows, sign_ref[...], preferred_element_type=jnp.float32) * scale
        return turned.astype(jnp.bfloat16)

    def spread(h):
        for which in range(2):
            turned = arrived(which, h)
            store[which, h, 0:blocks] = turned.reshape(blocks, block, HD)
            wide = turned.astype(jnp.float32)
            for i, slot in enumerate(slots):
                sent = picks[i][0] * wide[0:block]
                for j in range(1, blocks):
                    sent = sent + picks[i][j] * wide[j * block : (j + 1) * block]
                outbox[which, h, i] = sent.astype(jnp.bfloat16)
            for slot in slots:
                if_used(slot, lambda slot=slot, which=which: halo_copy(which, h, slot).start())

    position = lax.broadcasted_iota(jnp.int32, (block, HD), 0)

    def attend(h):
        query = arrived(2, h)
        for which in range(2):
            for slot in slots:
                if_used(slot, lambda slot=slot, which=which: halo_arrival(which, h, slot).wait_recv())
        keys = store[0, h].reshape(padded * block, HD)
        values = store[1, h].reshape(padded * block, HD)
        scores = lax.dot_general(
            query, keys, (((1,), (1,)), ((), ())), preferred_element_type=jnp.float32
        )
        halves, denominators = [], []
        for b in range(blocks):
            of_block = scores[b * block : (b + 1) * block] * scale + bias_ref[b : b + 1, :]
            peak = jnp.max(of_block, axis=1, keepdims=True)
            weights = jnp.exp(of_block - peak)
            denominators.append(jnp.sum(weights, axis=1, keepdims=True))
            halves.append(weights.astype(jnp.bfloat16))
        mixed = jnp.dot(
            jnp.concatenate(halves, axis=0), values, preferred_element_type=jnp.float32
        )
        mixed = mixed / jnp.concatenate(denominators, axis=0)
        first = mixed.astype(jnp.bfloat16)
        rest = mixed - first.astype(jnp.float32)
        second = rest.astype(jnp.bfloat16)
        third = (rest - second.astype(jnp.float32)).astype(jnp.bfloat16)
        sign = sign_ref[...]
        turned = jnp.dot(
            jnp.concatenate([first, second], axis=1),
            jnp.concatenate([sign, sign], axis=0),
            preferred_element_type=jnp.float32,
        )
        turned = turned + jnp.dot(third, sign, preferred_element_type=jnp.float32)
        turned = turned * scale
        for b in range(blocks):
            live = position < tokens_ref[me * blocks + b]
            result = jnp.where(live, turned[b * block : (b + 1) * block], 0.0)
            for owner in range(count_head):
                staged[h, owner, b] = result[owner * part : (owner + 1) * part].astype(jnp.bfloat16)
        for offset in reversed(range(1, count_head)):
            back_copy(offset, h).start()
        back_own(h).start()

    def step(h, carry):
        pl.when(h < heads)(lambda: spread(h))
        pl.when(h >= LEAD)(lambda: attend(h - LEAD))
        return carry

    lax.fori_loop(0, heads + LEAD, step, 0)

    def finish(h, carry):
        for which in range(3):
            for offset in reversed(range(1, count_head)):
                head_copy(which, offset, h).wait_send()
        for which in range(2):
            for slot in slots:
                if_used(slot, lambda slot=slot, which=which: halo_copy(which, h, slot).wait_send())
        for offset in reversed(range(1, count_head)):
            back_copy(offset, h).wait()
        back_own(h).wait()
        return carry

    lax.fori_loop(0, heads, finish, 0)


def shards(query_rows, key_rows, value_rows, pair_list, block_tokens):
    count_head = lax.axis_size("head")
    count_tm = lax.axis_size("tm")
    blocks, part, full_width = query_rows.shape
    block = part * count_head
    heads = full_width // (HD * count_head)
    total_blocks, listed = pair_list.shape
    slots = incoming_slots(count_tm)
    filled = blocks + len(slots)
    per_lane_tile = max(1, LANES // block)
    padded = -(-filled // per_lane_tile) * per_lane_tile
    shard_rows = -(-count_tm // 8) * 8
    sizes = (count_head, count_tm, blocks, part, heads, block, total_blocks, slots, padded)
    peers = max(1, count_head - 1)
    in_hbm = pl.BlockSpec(memory_space=pltpu.HBM)
    dma = pltpu.SemaphoreType.DMA
    return pl.pallas_call(
        functools.partial(kernel, sizes),
        out_shape=jax.ShapeDtypeStruct(query_rows.shape, jnp.bfloat16),
        in_specs=[in_hbm] * 5,
        out_specs=in_hbm,
        scratch_shapes=[
            pltpu.VMEM((3, heads, count_head, blocks, part, HD), jnp.bfloat16),
            pltpu.VMEM((2, heads, padded, block, HD), jnp.bfloat16),
            pltpu.VMEM((2, heads, len(slots), block, HD), jnp.bfloat16),
            pltpu.VMEM((heads, count_head, blocks, part, HD), jnp.bfloat16),
            pltpu.VMEM((total_blocks, listed), jnp.int32),
            pltpu.SMEM((total_blocks,), jnp.int32),
            pltpu.VMEM((count_tm, blocks, LANES), jnp.float32),
            pltpu.VMEM((NEAR_CAP, count_tm, 1, LANES), jnp.float32),
            pltpu.VMEM((shard_rows, LANES), jnp.float32),
            pltpu.VMEM((blocks, padded * block), jnp.float32),
            pltpu.VMEM((HD, HD), jnp.bfloat16),
            dma((3, peers, heads)),
            dma((3, peers, heads)),
            dma((3, heads)),
            dma((2, heads, len(slots))),
            dma((2, heads, len(slots))),
            dma((peers, heads)),
            dma((peers, heads)),
            dma((heads,)),
            dma(()),
            dma(()),
        ],
        compiler_params=pltpu.CompilerParams(
            collective_id=0, has_side_effects=True, vmem_limit_bytes=32 * 1024 * 1024
        ),
    )(*[pltpu.with_memory_space_constraint(x, pltpu.HBM) for x in (query_rows, key_rows, value_rows, pair_list, block_tokens)])


def solution(mesh):
    placed = (
        P(("grp", "tm"), "head", None),
        P(("grp", "tm"), "head", None),
        P(("grp", "tm"), "head", None),
        P("grp", None),
        P("grp"),
    )
    return jax.shard_map(
        shards,
        mesh=mesh,
        in_specs=placed,
        out_specs=P(("grp", "tm"), "head", None),
        check_vma=False,
    )
```

profile of v0, /device:TPU:0, one launch (start us, length us, event | category | flops | bytes accessed | tf_op | source)
XLA Modules:
  0.0 43.9 jit_solution(4529268935834070542)
XLA Ops:
  0.0 43.1 %shard_map.55 = bf16[4,16,3072]{2,1,0:T(8,128)(2,1)S(1)} custom-call(bf16[4,16,3072]{2,1,0:T(8,128)(2,1)} %query_ref.1, bf16[4,16,3072]{2,1,0:T(8,128)(2,1)} %key_ref.1, bf16[4,16,3072]{2,1,0:T(8,128)(2,1)} %value_ref.1, s32[16,32]{1,0:T(8,128)} %pair_ref.1, s32[16]{0:T(128)} %tokens_far.1), custom_call_target="tpu_custom_call" | custom-call | tf_op jit(solution)/shard_map/pallas_call | solution.py:364
  43.1 0.7 %copy.7 = bf16[4,16,3072]{2,1,0:T(8,128)(2,1)} copy(bf16[4,16,3072]{2,1,0:T(8,128)(2,1)S(1)} %shard_map.55) | data formatting | bytes 786432
where the time goes:
time: 44 us; the launch traced here: 43.9 us
  Pallas kernels  43.1 us (98%)
  local copies, waits for them, and re-layouts  0.75 us (2%)
    pallas_call x1, Pallas kernels, shards(): pl.pallas_call(functools.partial(kernel, sizes), out_shape=jax.ShapeDtype...  43.1 us

commit v1 on v0

--- a/solution.py
+++ b/solution.py
@@ -12,7 +12,8 @@
 NEAR_CAP = 2
 FAR_CAP = 1
 LANES = 128
-LEAD = 2
+PAIR_HEADS = 3
+QUERY_HEADS = 1
 MESH = pl.DeviceIdType.MESH
 
 
@@ -34,6 +35,18 @@
     return index
 
 
+def heads_together(heads, most):
+    return max(size for size in range(1, most + 1) if heads % size == 0)
+
+
+def sending_order(count):
+    order, top = [], 1
+    while top < count:
+        order = list(range(top, min(2 * top, count))) + order
+        top *= 2
+    return order
+
+
 def sign_table(dimension):
     rows = lax.broadcasted_iota(jnp.int32, (dimension, dimension), 0)
     columns = lax.broadcasted_iota(jnp.int32, (dimension, dimension), 1)
@@ -52,7 +65,8 @@
     pair_ref,
     tokens_far,
     out_ref,
-    gathered,
+    pair_in,
+    query_in,
     store,
     outbox,
     staged,
@@ -63,9 +77,14 @@
     wanted_ref,
     bias_ref,
     sign_ref,
-    head_send,
-    head_recv,
-    local_sem,
+    pair_send,
+    pair_recv,
+    query_send,
+    query_recv,
+    pair_local,
+    query_local,
+    entered_low,
+    entered_high,
     halo_send,
     halo_recv,
     back_send,
@@ -74,127 +93,168 @@
     pair_sem,
     tokens_sem,
 ):
-    count_head, count_tm, blocks, part, heads, block, total_blocks, slots, padded = sizes
+    count_head, count_tm, blocks, part, heads, block, total_blocks, slots, padded, grouped = sizes
+    pair_heads, query_heads = grouped
+    pair_groups, query_groups = heads // pair_heads, heads // query_heads
     width = heads * HD
     my_head = lax.axis_index("head")
     me = lax.axis_index("tm")
     scale = 1.0 / math.sqrt(HD)
     slot_of = {slot: i for i, slot in enumerate(slots)}
-    sources = (key_ref, value_ref, query_ref)
-
-    for offset in reversed(range(1, count_head)):
+    order = sending_order(count_head)
+
+    def columns_of(owner, first, count):
+        return pl.ds(pl.multiple_of(owner * width + first * HD, HD), count * HD)
+
+    def head_copy(which, offset, g):
         peer = partner(my_head, offset, count_head)
-        pl.semaphore_signal(
-            pltpu.get_barrier_semaphore(), inc=1, device_id={"head": peer}, device_id_type=MESH
-        )
-
-    def columns_of(owner, h):
-        return pl.ds(pl.multiple_of(owner * width + h * HD, HD), HD)
-
-    def head_copy(which, offset, h):
-        peer = partner(my_head, offset, count_head)
+        if which < 2:
+            return pltpu.make_async_remote_copy(
+                src_ref=(key_ref, value_ref)[which].at[
+                    :, :, columns_of(peer, g * pair_heads, pair_heads)
+                ],
+                dst_ref=pair_in.at[which, g, my_head],
+                send_sem=pair_send.at[which, offset - 1, g],
+                recv_sem=pair_recv.at[which, offset - 1, g],
+                device_id={"head": peer},
+                device_id_type=MESH,
+            )
         return pltpu.make_async_remote_copy(
-            src_ref=sources[which].at[:, :, columns_of(peer, h)],
-            dst_ref=gathered.at[which, h, my_head],
-            send_sem=head_send.at[which, offset - 1, h],
-            recv_sem=head_recv.at[which, offset - 1, h],
+            src_ref=query_ref.at[:, :, columns_of(peer, g * query_heads, query_heads)],
+            dst_ref=query_in.at[g, my_head],
+            send_sem=query_send.at[offset - 1, g],
+            recv_sem=query_recv.at[offset - 1, g],
             device_id={"head": peer},
             device_id_type=MESH,
         )
 
-    def local_copy(which, h):
+    def local_copy(which, g):
+        if which < 2:
+            return pltpu.make_async_copy(
+                (key_ref, value_ref)[which].at[
+                    :, :, columns_of(my_head, g * pair_heads, pair_heads)
+                ],
+                pair_in.at[which, g, my_head],
+                pair_local.at[which, g],
+            )
         return pltpu.make_async_copy(
-            sources[which].at[:, :, columns_of(my_head, h)],
-            gathered.at[which, h, my_head],
-            local_sem.at[which, h],
-        )
-
-    def halo_copy(which, h, slot):
+            query_ref.at[:, :, columns_of(my_head, g * query_heads, query_heads)],
+            query_in.at[g, my_head],
+            query_local.at[g],
+        )
+
+    def halo_copy(which, g, slot):
         offset, place = slot
         peer = lax.rem(me + offset, count_tm)
         landing = slot_of[(count_tm - offset, place)]
         return pltpu.make_async_remote_copy(
-            src_ref=outbox.at[which, h, slot_of[slot]],
-            dst_ref=store.at[which, h, blocks + landing],
-            send_sem=halo_send.at[which, h, slot_of[slot]],
-            recv_sem=halo_recv.at[which, h, landing],
+            src_ref=outbox.at[which, g, slot_of[slot]],
+            dst_ref=store.at[which, pl.ds(g * pair_heads, pair_heads), blocks + landing],
+            send_sem=halo_send.at[which, g, slot_of[slot]],
+            recv_sem=halo_recv.at[which, g, landing],
             device_id={"tm": peer},
             device_id_type=MESH,
         )
 
-    def halo_arrival(which, h, slot):
+    def halo_arrival(which, g, slot):
         i = slot_of[slot]
         peer = lax.rem(me + slot[0], count_tm)
         return pltpu.make_async_remote_copy(
-            src_ref=outbox.at[which, h, i],
-            dst_ref=store.at[which, h, blocks + i],
-            send_sem=halo_send.at[which, h, i],
-            recv_sem=halo_recv.at[which, h, i],
+            src_ref=outbox.at[which, g, i],
+            dst_ref=store.at[which, pl.ds(g * pair_heads, pair_heads), blocks + i],
+            send_sem=halo_send.at[which, g, i],
+            recv_sem=halo_recv.at[which, g, i],
             device_id={"tm": peer},
             device_id_type=MESH,
         )
+
+    def beside(slot):
+        peer = lax.rem(me + slot[0], count_tm)
+        return (peer == me + 1) | (peer == me - 1)
 
     def if_used(slot, action):
         if slot[1] < FAR_CAP:
             action()
         else:
-            peer = lax.rem(me + slot[0], count_tm)
-            near = (peer == me + 1) | (peer == me - 1)
-            pl.when(near)(action)
-
-    def back_copy(offset, h):
+            pl.when(beside(slot))(action)
+
+    def back_copy(offset, g):
         peer = partner(my_head, offset, count_head)
         return pltpu.make_async_remote_copy(
-            src_ref=staged.at[h, peer],
-            dst_ref=out_ref.at[:, :, columns_of(my_head, h)],
-            send_sem=back_send.at[offset - 1, h],
-            recv_sem=back_recv.at[offset - 1, h],
+            src_ref=staged.at[g, peer],
+            dst_ref=out_ref.at[:, :, columns_of(my_head, g * query_heads, query_heads)],
+            send_sem=back_send.at[offset - 1, g],
+            recv_sem=back_recv.at[offset - 1, g],
             device_id={"head": peer},
             device_id_type=MESH,
         )
 
-    def back_own(h):
+    def back_own(g):
         return pltpu.make_async_copy(
-            staged.at[h, my_head],
-            out_ref.at[:, :, columns_of(my_head, h)],
-            back_local.at[h],
-        )
-
-    store[:, :, blocks:] = jnp.zeros((2, heads, padded - blocks, block, HD), jnp.bfloat16)
+            staged.at[g, my_head],
+            out_ref.at[:, :, columns_of(my_head, g * query_heads, query_heads)],
+            back_local.at[g],
+        )
+
+    def greet(axis, peer):
+        pl.semaphore_signal(
+            pltpu.get_barrier_semaphore(), inc=1, device_id={axis: peer}, device_id_type=MESH
+        )
+
+    def tell(semaphore, peer):
+        pl.semaphore_signal(semaphore, inc=1, device_id={"head": peer}, device_id_type=MESH)
+
+    has_low, has_high = my_head > 0, my_head < count_head - 1
+    pl.when(has_low)(lambda: greet("head", my_head - 1))
+    pl.when(has_high)(lambda: greet("head", my_head + 1))
     for offset in range(1, count_tm):
-        peer = lax.rem(me + offset, count_tm)
-        pl.semaphore_signal(
-            pltpu.get_barrier_semaphore(), inc=1, device_id={"tm": peer}, device_id_type=MESH
-        )
+        greet("tm", lax.rem(me + offset, count_tm))
     pair_copy = pltpu.make_async_copy(pair_ref, pair_here, pair_sem)
     pair_copy.start()
     tokens_copy = pltpu.make_async_copy(tokens_far, tokens_ref, tokens_sem)
     tokens_copy.start()
-
+    for which, groups in ((0, pair_groups), (1, pair_groups), (2, query_groups)):
+        for g in range(groups):
+            local_copy(which, g).start()
+
+    def clear(i):
+        store[:, :, i] = jnp.zeros((2, heads, block, HD), jnp.bfloat16)
+
+    for i, slot in enumerate(slots):
+        if slot[1] >= FAR_CAP:
+            pl.when(jnp.logical_not(beside(slot)))(lambda i=i: clear(blocks + i))
+    for i in range(blocks + len(slots), padded):
+        clear(i)
     sign_ref[...] = sign_table(HD).astype(jnp.bfloat16)
-    pl.semaphore_wait(pltpu.get_barrier_semaphore(), count_head - 1 + count_tm - 1)
-
-    def start_remote(which, h):
-        for offset in reversed(range(1, count_head)):
-            head_copy(which, offset, h).start()
-
-    def start_step(h, carry):
-        @pl.when(h < heads)
-        def _():
-            start_remote(0, h)
-            start_remote(1, h)
-
-        pl.when(h >= LEAD)(lambda: start_remote(2, h - LEAD))
-        return carry
-
-    lax.fori_loop(0, heads + LEAD, start_step, 0)
-
-    def start_local(h, carry):
-        for which in range(3):
-            local_copy(which, h).start()
-        return carry
-
-    lax.fori_loop(0, heads, start_local, 0)
+
+    neighbours = jnp.where(has_low, 1, 0) + jnp.where(has_high, 1, 0)
+    pl.semaphore_wait(pltpu.get_barrier_semaphore(), neighbours + count_tm - 1)
+
+    def start_at(distance):
+        for offset in order:
+            peer = partner(my_head, offset, count_head)
+            here = (peer == my_head + distance) | (peer == my_head - distance)
+            pl.when(here)(lambda offset=offset: head_copy(0, offset, 0).start())
+
+    for distance in range(1, count_head):
+        if distance > 1:
+            seen_low, seen_high = my_head >= distance - 1, my_head <= count_head - distance
+            low, high = entered_low.at[distance - 2], entered_high.at[distance - 2]
+            pl.when(seen_low & has_high)(lambda low=low: tell(low, my_head + 1))
+            pl.when(seen_high & has_low)(lambda high=high: tell(high, my_head - 1))
+            pl.when(my_head >= distance)(lambda low=low: pl.semaphore_wait(low, 1))
+            pl.when(my_head <= count_head - 1 - distance)(
+                lambda high=high: pl.semaphore_wait(high, 1)
+            )
+        start_at(distance)
+    for g in range(pair_groups):
+        for which in range(2):
+            if (which, g) != (0, 0):
+                for offset in order:
+                    head_copy(which, offset, g).start()
+    for g in range(query_groups):
+        for offset in order:
+            head_copy(2, offset, g).start()
 
     pair_copy.wait()
     tokens_copy.wait()
@@ -252,40 +312,44 @@
         key_end = key_end + inside * (kept + float(i * block))
     bias_ref[...] = jnp.where(key_lane.astype(jnp.float32) < key_end, 0.0, -1e30)
 
-    def arrived(which, h):
-        local_copy(which, h).wait()
-        for offset in reversed(range(1, count_head)):
-            head_copy(which, offset, h).wait_recv()
+    def arrived(which, g):
+        local_copy(which, g).wait()
+        for offset in order:
+            head_copy(which, offset, g).wait_recv()
+
+    def rotated(landed, column):
+        lanes = pl.ds(pl.multiple_of(column * HD, HD), HD)
         rows = jnp.concatenate(
-            [
-                gathered[which, h, :, b].astype(jnp.float32).reshape(block, HD)
-                for b in range(blocks)
-            ],
+            [landed[:, b, :, lanes].astype(jnp.float32).reshape(block, HD) for b in range(blocks)],
             axis=0,
         ).astype(jnp.bfloat16)
         turned = jnp.dot(rows, sign_ref[...], preferred_element_type=jnp.float32) * scale
         return turned.astype(jnp.bfloat16)
 
-    def spread(h):
-        for which in range(2):
-            turned = arrived(which, h)
+    def spread(which, g):
+        arrived(which, g)
+
+        def one_head(column, carry):
+            h = g * pair_heads + column
+            turned = rotated(pair_in.at[which, g], column)
             store[which, h, 0:blocks] = turned.reshape(blocks, block, HD)
             wide = turned.astype(jnp.float32)
             for i, slot in enumerate(slots):
                 sent = picks[i][0] * wide[0:block]
                 for j in range(1, blocks):
                     sent = sent + picks[i][j] * wide[j * block : (j + 1) * block]
-                outbox[which, h, i] = sent.astype(jnp.bfloat16)
-            for slot in slots:
-                if_used(slot, lambda slot=slot, which=which: halo_copy(which, h, slot).start())
+                outbox[which, g, i, column] = sent.astype(jnp.bfloat16)
+            return carry
+
+        lax.fori_loop(0, pair_heads, one_head, 0)
+        for slot in slots:
+            if_used(slot, lambda slot=slot: halo_copy(which, g, slot).start())
 
     position = lax.broadcasted_iota(jnp.int32, (block, HD), 0)
 
-    def attend(h):
-        query = arrived(2, h)
-        for which in range(2):
-            for slot in slots:
-                if_used(slot, lambda slot=slot, which=which: halo_arrival(which, h, slot).wait_recv())
+    def attend(g, column):
+        h = g * query_heads + column
+        query = rotated(query_in.at[g], column)
         keys = store[0, h].reshape(padded * block, HD)
         values = store[1, h].reshape(padded * block, HD)
         scores = lax.dot_general(
@@ -318,31 +382,51 @@
             live = position < tokens_ref[me * blocks + b]
             result = jnp.where(live, turned[b * block : (b + 1) * block], 0.0)
             for owner in range(count_head):
-                staged[h, owner, b] = result[owner * part : (owner + 1) * part].astype(jnp.bfloat16)
-        for offset in reversed(range(1, count_head)):
-            back_copy(offset, h).start()
-        back_own(h).start()
-
-    def step(h, carry):
-        pl.when(h < heads)(lambda: spread(h))
-        pl.when(h >= LEAD)(lambda: attend(h - LEAD))
+                staged[g, owner, b, :, column * HD : (column + 1) * HD] = result[
+                    owner * part : (owner + 1) * part
+                ].astype(jnp.bfloat16)
+
+    def spread_group(g, carry):
+        spread(0, g)
+        spread(1, g)
         return carry
 
-    lax.fori_loop(0, heads + LEAD, step, 0)
-
-    def finish(h, carry):
-        for which in range(3):
-            for offset in reversed(range(1, count_head)):
-                head_copy(which, offset, h).wait_send()
+    lax.fori_loop(0, pair_groups, spread_group, 0)
+
+    def attend_group(g, carry):
+        arrived(2, g)
+
+        def halos():
+            for which in range(2):
+                for slot in slots:
+                    if_used(
+                        slot,
+                        lambda slot=slot, which=which: halo_arrival(
+                            which, lax.div(g * query_heads, pair_heads), slot
+                        ).wait_recv(),
+                    )
+
+        pl.when(lax.rem(g * query_heads, pair_heads) == 0)(halos)
+        for column in range(query_heads):
+            attend(g, column)
+        for offset in order:
+            back_copy(offset, g).start()
+        back_own(g).start()
+        return carry
+
+    lax.fori_loop(0, query_groups, attend_group, 0)
+
+    for g in range(pair_groups):
         for which in range(2):
+            for offset in order:
+                head_copy(which, offset, g).wait_send()
             for slot in slots:
-                if_used(slot, lambda slot=slot, which=which: halo_copy(which, h, slot).wait_send())
-        for offset in reversed(range(1, count_head)):
-            back_copy(offset, h).wait()
-        back_own(h).wait()
-        return carry
-
-    lax.fori_loop(0, heads, finish, 0)
+                if_used(slot, lambda slot=slot, which=which: halo_copy(which, g, slot).wait_send())
+    for g in range(query_groups):
+        for offset in order:
+            head_copy(2, offset, g).wait_send()
+            back_copy(offset, g).wait()
+        back_own(g).wait()
 
 
 def shards(query_rows, key_rows, value_rows, pair_list, block_tokens):
@@ -357,8 +441,15 @@
     per_lane_tile = max(1, LANES // block)
     padded = -(-filled // per_lane_tile) * per_lane_tile
     shard_rows = -(-count_tm // 8) * 8
-    sizes = (count_head, count_tm, blocks, part, heads, block, total_blocks, slots, padded)
+    pair_heads = heads_together(heads, PAIR_HEADS)
+    query_heads = heads_together(pair_heads, QUERY_HEADS)
+    pair_groups, query_groups = heads // pair_heads, heads // query_heads
+    grouped = (pair_heads, query_heads)
+    sizes = (
+        count_head, count_tm, blocks, part, heads, block, total_blocks, slots, padded, grouped
+    )
     peers = max(1, count_head - 1)
+    rounds = max(1, count_head - 2)
     in_hbm = pl.BlockSpec(memory_space=pltpu.HBM)
     dma = pltpu.SemaphoreType.DMA
     return pl.pallas_call(
@@ -367,10 +458,13 @@
         in_specs=[in_hbm] * 5,
         out_specs=in_hbm,
         scratch_shapes=[
-            pltpu.VMEM((3, heads, count_head, blocks, part, HD), jnp.bfloat16),
+            pltpu.VMEM(
+                (2, pair_groups, count_head, blocks, part, pair_heads * HD), jnp.bfloat16
+            ),
+            pltpu.VMEM((query_groups, count_head, blocks, part, query_heads * HD), jnp.bfloat16),
             pltpu.VMEM((2, heads, padded, block, HD), jnp.bfloat16),
-            pltpu.VMEM((2, heads, len(slots), block, HD), jnp.bfloat16),
-            pltpu.VMEM((heads, count_head, blocks, part, HD), jnp.bfloat16),
+            pltpu.VMEM((2, pair_groups, len(slots), pair_heads, block, HD), jnp.bfloat16),
+            pltpu.VMEM((query_groups, count_head, blocks, part, query_heads * HD), jnp.bfloat16),
             pltpu.VMEM((total_blocks, listed), jnp.int32),
             pltpu.SMEM((total_blocks,), jnp.int32),
             pltpu.VMEM((count_tm, blocks, LANES), jnp.float32),
@@ -378,14 +472,19 @@
             pltpu.VMEM((shard_rows, LANES), jnp.float32),
             pltpu.VMEM((blocks, padded * block), jnp.float32),
             pltpu.VMEM((HD, HD), jnp.bfloat16),
-            dma((3, peers, heads)),
-            dma((3, peers, heads)),
-            dma((3, heads)),
-            dma((2, heads, len(slots))),
-            dma((2, heads, len(slots))),
-            dma((peers, heads)),
-            dma((peers, heads)),
-            dma((heads,)),
+            dma((2, peers, pair_groups)),
+            dma((2, peers, pair_groups)),
+            dma((peers, query_groups)),
+            dma((peers, query_groups)),
+            dma((2, pair_groups)),
+            dma((query_groups,)),
+            pltpu.SemaphoreType.REGULAR((rounds,)),
+            pltpu.SemaphoreType.REGULAR((rounds,)),
+            dma((2, pair_groups, len(slots))),
+            dma((2, pair_groups, len(slots))),
+            dma((peers, query_groups)),
+            dma((peers, query_groups)),
+            dma((query_groups,)),
             dma(()),
             dma(()),
         ],

time: 44 us -> 42.6 us (0.968)
  Pallas kernels: 43.1 us -> 41.7 us
    pallas_call x1, Pallas kernels: 43.1 us -> 41.7 us  [shards(): pl.pallas_call(functools.partial(kernel, sizes), out_shape=jax.ShapeDtype...]
where the time goes in v1:
time: 42.6 us; the launch traced here: 42.4 us
  Pallas kernels  41.7 us (98%)
  local copies, waits for them, and re-layouts  0.75 us (2%)
    pallas_call x1, Pallas kernels, shards(): pl.pallas_call(functools.partial(kernel, sizes), out_shape=jax.ShapeDtype...  41.7 us

profile of v1, /device:TPU:0, one launch (start us, length us, event | category | flops | bytes accessed | tf_op | source)
XLA Modules:
  0.0 42.4 jit_solution(7264116456549290423)
XLA Ops:
  0.0 41.7 %shard_map.55 = bf16[4,16,3072]{2,1,0:T(8,128)(2,1)S(1)} custom-call(bf16[4,16,3072]{2,1,0:T(8,128)(2,1)} %query_ref.1, bf16[4,16,3072]{2,1,0:T(8,128)(2,1)} %key_ref.1, bf16[4,16,3072]{2,1,0:T(8,128)(2,1)} %value_ref.1, s32[16,32]{1,0:T(8,128)} %pair_ref.1, s32[16]{0:T(128)} %tokens_far.1), custom_call_target="tpu_custom_call" | custom-call | tf_op jit(solution)/shard_map/pallas_call | solution.py:455
  41.7 0.7 %copy.7 = bf16[4,16,3072]{2,1,0:T(8,128)(2,1)} copy(bf16[4,16,3072]{2,1,0:T(8,128)(2,1)S(1)} %shard_map.55) | data formatting | bytes 786432

commit v2 on v1

v2 whole, which is shorter than its diff:
```python
import functools
import math

import jax
import jax.numpy as jnp
from jax import lax
from jax.experimental import pallas as pl
from jax.experimental.pallas import tpu as pltpu
from jax.sharding import PartitionSpec as P

HD = 128
NEAR_CAP = 2
FAR_CAP = 1
LANES = 128
EARLY = 2
DEFER = 0
PAIRS_BY_PEER = False
QUERIES_BY_PEER = False
KEY_HEADS = 3
VALUE_HEADS = 3
QUERY_HEADS = 3
MESH = pl.DeviceIdType.MESH


def incoming_slots(count_tm):
    slots = []
    for offset in range(1, count_tm):
        capacity = NEAR_CAP if offset in (1, count_tm - 1) else FAR_CAP
        slots += [(offset, place) for place in range(capacity)]
    return slots


def heads_together(heads, most):
    return max(size for size in range(1, most + 1) if heads % size == 0)


def sign_table(dimension):
    rows = lax.broadcasted_iota(jnp.int32, (dimension, dimension), 0)
    columns = lax.broadcasted_iota(jnp.int32, (dimension, dimension), 1)
    common = rows & columns
    parity = jnp.zeros((dimension, dimension), jnp.int32)
    for bit_level in range(dimension.bit_length() - 1):
        parity = parity + ((common >> bit_level) & 1)
    return jnp.where((parity & 1) == 0, 1.0, -1.0).astype(jnp.float32)


def kernel(
    sizes,
    query_ref,
    key_ref,
    value_ref,
    pair_ref,
    tokens_far,
    out_ref,
    key_in,
    value_in,
    query_in,
    store,
    key_outbox,
    value_outbox,
    key_halo,
    value_halo,
    staged,
    pair_here,
    tokens_ref,
    listed_ref,
    place_ref,
    wanted_ref,
    bias_ref,
    sign_ref,
    head_send,
    head_recv,
    head_local,
    entered_low,
    entered_high,
    column_up,
    column_side,
    column_down,
    halo_send,
    halo_recv,
    back_send,
    back_recv,
    back_local,
    pair_sem,
    tokens_sem,
):
    count_head, count_tm, blocks, part, heads, block, total_blocks, slots, padded, grouped = sizes
    sources, landed = (key_ref, value_ref, query_ref), (key_in, value_in, query_in)
    outbox, halo = (key_outbox, value_outbox), (key_halo, value_halo)
    groups = [heads // size for size in grouped]
    query_heads, query_groups = grouped[2], groups[2]
    offsets = range(1, count_tm)
    places = {o: [p for k, p in slots if k == o] for o in offsets}
    width = heads * HD
    my_head = lax.axis_index("head")
    me = lax.axis_index("tm")
    scale = 1.0 / math.sqrt(HD)
    slot_of = {slot: i for i, slot in enumerate(slots)}
    others = [k + jnp.where(my_head <= k, 1, 0) for k in range(count_head - 1)]
    upper_half = my_head >= count_head // 2
    far_first = [
        jnp.where(upper_half, low, high) for low, high in zip(others, reversed(others))
    ]

    def columns_of(owner, first, count):
        return pl.ds(pl.multiple_of(owner * width + first * HD, HD), count * HD)

    def head_copy(which, peer, g, source=None):
        source = my_head if source is None else source
        return pltpu.make_async_remote_copy(
            src_ref=sources[which].at[:, :, columns_of(peer, g * grouped[which], grouped[which])],
            dst_ref=landed[which].at[g, source],
            send_sem=head_send.at[which, peer, g],
            recv_sem=head_recv.at[which, source, g],
            device_id={"head": peer},
            device_id_type=MESH,
        )

    def local_copy(which, g):
        return pltpu.make_async_copy(
            sources[which].at[:, :, columns_of(my_head, g * grouped[which], grouped[which])],
            landed[which].at[g, my_head],
            head_local.at[which, g],
        )

    def halo_copy(which, g, offset, count, arriving=False):
        peer = lax.rem(me + offset, count_tm)
        first = slot_of[(offset, 0)]
        landing = first if arriving else slot_of[(count_tm - offset, 0)]
        return pltpu.make_async_remote_copy(
            src_ref=outbox[which].at[g, pl.ds(first, count)],
            dst_ref=halo[which].at[g, pl.ds(landing, count)],
            send_sem=halo_send.at[which, g, offset - 1],
            recv_sem=halo_recv.at[which, g, (offset if arriving else count_tm - offset) - 1],
            device_id={"tm": peer},
            device_id_type=MESH,
        )

    def beside(offset):
        peer = lax.rem(me + offset, count_tm)
        return (peer == me + 1) | (peer == me - 1)

    def each_halo(which, g, action, arriving=False):
        for offset in offsets:
            full = len(places[offset])
            if full == FAR_CAP:
                action(halo_copy(which, g, offset, full, arriving))
            else:
                near = beside(offset)
                pl.when(near)(lambda o=offset, n=full: action(halo_copy(which, g, o, n, arriving)))
                pl.when(jnp.logical_not(near))(
                    lambda o=offset: action(halo_copy(which, g, o, FAR_CAP, arriving))
                )

    def back_copy(peer, g, source=None):
        source = my_head if source is None else source
        return pltpu.make_async_remote_copy(
            src_ref=staged.at[g, peer],
            dst_ref=out_ref.at[:, :, columns_of(source, g * query_heads, query_heads)],
            send_sem=back_send.at[peer, g],
            recv_sem=back_recv.at[source, g],
            device_id={"head": peer},
            device_id_type=MESH,
        )

    def back_own(g):
        return pltpu.make_async_copy(
            staged.at[g, my_head],
            out_ref.at[:, :, columns_of(my_head, g * query_heads, query_heads)],
            back_local.at[g],
        )

    def greet(axis, peer):
        pl.semaphore_signal(
            pltpu.get_barrier_semaphore(), inc=1, device_id={axis: peer}, device_id_type=MESH
        )

    def tell(semaphore, peer):
        pl.semaphore_signal(semaphore, inc=1, device_id={"head": peer}, device_id_type=MESH)

    has_low, has_high = my_head > 0, my_head < count_head - 1
    pl.when(has_low)(lambda: greet("head", my_head - 1))
    pl.when(has_high)(lambda: greet("head", my_head + 1))
    hub = my_head == 0

    @pl.when(hub)
    def _():
        for offset in range(1, count_tm):
            greet("tm", lax.rem(me + offset, count_tm))

    pair_copy = pltpu.make_async_copy(pair_ref, pair_here, pair_sem)
    pair_copy.start()
    tokens_copy = pltpu.make_async_copy(tokens_far, tokens_ref, tokens_sem)
    tokens_copy.start()
    for which in range(3):
        for g in range(groups[which]):
            local_copy(which, g).start()

    def clear(i):
        for which in range(2):
            shape = (groups[which], grouped[which], block, HD)
            halo[which][:, i] = jnp.zeros(shape, jnp.bfloat16)

    for i, (offset, place) in enumerate(slots):
        if place >= FAR_CAP:
            pl.when(jnp.logical_not(beside(offset)))(lambda i=i: clear(i))
    sign_ref[...] = sign_table(HD).astype(jnp.bfloat16)

    neighbours = jnp.where(has_low, 1, 0) + jnp.where(has_high, 1, 0)
    awaited = neighbours + jnp.where(hub, count_tm - 1, 0)
    pl.semaphore_wait(pltpu.get_barrier_semaphore(), awaited)

    pairs_of = sorted(
        ((which, g) for which in range(2) for g in range(groups[which])),
        key=lambda piece: piece[1] * grouped[piece[0]],
    )
    queries_of = [(2, g) for g in range(query_groups)]
    early = pairs_of[:EARLY]

    def start_at(distance):
        for side in (-distance, distance):
            peer = my_head + side
            inside = (peer >= 0) & (peer < count_head)
            for which, g in early:
                pl.when(inside)(lambda p=peer, w=which, g=g: head_copy(w, p, g).start())

    for distance in range(1, count_head):
        if distance > 1:
            seen_low, seen_high = my_head >= distance - 1, my_head <= count_head - distance
            low, high = entered_low.at[distance - 2], entered_high.at[distance - 2]
            pl.when(seen_low & has_high)(lambda low=low: tell(low, my_head + 1))
            pl.when(seen_high & has_low)(lambda high=high: tell(high, my_head - 1))
            pl.when(my_head >= distance)(lambda low=low: pl.semaphore_wait(low, 1))
            pl.when(my_head <= count_head - 1 - distance)(
                lambda high=high: pl.semaphore_wait(high, 1)
            )
        start_at(distance)
    pl.when(my_head < count_head - 1)(lambda: pl.semaphore_wait(column_up, 1))
    pl.when(has_low)(lambda: tell(column_up, my_head - 1))

    for pieces, by_peer in ((pairs_of, PAIRS_BY_PEER), (queries_of, QUERIES_BY_PEER)):
        if by_peer:
            plan = [(piece, peer) for peer in far_first for piece in pieces]
        else:
            plan = [(piece, peer) for piece in pieces for peer in far_first]
        for (which, g), peer in plan:
            if (which, g) not in early:
                head_copy(which, peer, g).start()

    @pl.when(hub)
    def _():
        for offset in range(1, count_tm):
            pl.semaphore_signal(
                column_side,
                inc=1,
                device_id={"tm": lax.rem(me + offset, count_tm)},
                device_id_type=MESH,
            )

    pair_copy.wait()
    tokens_copy.wait()
    pairs = pair_here[...]
    lane = lax.broadcasted_iota(jnp.int32, (1, LANES), 1)
    listed = jnp.zeros((total_blocks, LANES), jnp.float32)
    token_row = jnp.zeros((1, LANES), jnp.float32)
    for k in range(total_blocks):
        found = jnp.max(jnp.where(pairs == k, 1.0, 0.0), axis=1, keepdims=True)
        here = jnp.where(lane == k, 1.0, 0.0)
        listed = listed + found * here
        token_row = token_row + here * tokens_ref[k].astype(jnp.float32)
    wanted_ref[...] = jnp.zeros_like(wanted_ref)
    for t in range(count_tm):
        of_shard = listed[t * blocks : (t + 1) * blocks]
        listed_ref[t] = of_shard
        wanted_ref[t : t + 1, :] = jnp.max(of_shard, axis=0, keepdims=True)
    low = lax.broadcasted_iota(jnp.int32, (LANES, LANES), 0)
    high = lax.broadcasted_iota(jnp.int32, (LANES, LANES), 1)
    low_shard, high_shard = jnp.zeros_like(low), jnp.zeros_like(high)
    lane_shard = jnp.zeros_like(lane)
    for t in range(1, count_tm):
        low_shard = low_shard + jnp.where(low >= t * blocks, 1, 0)
        high_shard = high_shard + jnp.where(high >= t * blocks, 1, 0)
        lane_shard = lane_shard + jnp.where(lane >= t * blocks, 1, 0)
    before = jnp.where((low_shard == high_shard) & (low < high), 1.0, 0.0).astype(jnp.bfloat16)
    wanted = wanted_ref[...]
    rank = jnp.dot(wanted.astype(jnp.bfloat16), before, preferred_element_type=jnp.float32)
    for place in range(NEAR_CAP):
        chosen = jnp.where(rank == float(place), wanted, 0.0)
        for t in range(count_tm):
            place_ref[place, t] = chosen[t : t + 1, :]
    picks = []
    for offset, place in slots:
        row = place_ref[place, lax.rem(me + offset, count_tm)]
        picks.append(
            [
                jnp.sum(jnp.where(lane == me * blocks + j, row, 0.0), axis=1, keepdims=True)
                for j in range(blocks)
            ]
        )
    mine = listed_ref[me]
    key_lane = lax.broadcasted_iota(jnp.int32, (1, padded * block), 1)
    key_end = jnp.zeros((blocks, padded * block), jnp.float32)
    for i in range(blocks + len(slots)):
        if i < blocks:
            kept_tokens = jnp.where(lane == me * blocks + i, token_row, 0.0)
        else:
            offset, place = slots[i - blocks]
            owner = lax.rem(me + offset, count_tm)
            row = place_ref[place, me]
            kept_tokens = jnp.where(lane_shard == owner, row * token_row, 0.0)
        kept = jnp.sum(mine * kept_tokens, axis=1, keepdims=True)
        inside = jnp.where((key_lane >= i * block) & (key_lane < (i + 1) * block), 1.0, 0.0)
        key_end = key_end + inside * (kept + float(i * block))
    bias_ref[...] = jnp.where(key_lane.astype(jnp.float32) < key_end, 0.0, -1e30)

    def arrived(which, g):
        local_copy(which, g).wait()
        for peer in others:
            head_copy(which, peer, g, source=peer).wait_recv()

    def rotated(which, g, column):
        lanes = pl.ds(pl.multiple_of(column * HD, HD), HD)
        rows = jnp.concatenate(
            [
                landed[which][g, :, b, :, lanes].astype(jnp.float32).reshape(block, HD)
                for b in range(blocks)
            ],
            axis=0,
        ).astype(jnp.bfloat16)
        turned = jnp.dot(rows, sign_ref[...], preferred_element_type=jnp.float32) * scale
        return turned.astype(jnp.bfloat16)

    def spread(which, g):
        arrived(which, g)

        def one_head(column, carry):
            turned = rotated(which, g, column)
            store[which, g * grouped[which] + column] = turned
            wide = turned.astype(jnp.float32)
            for i in range(len(slots)):
                sent = picks[i][0] * wide[0:block]
                for j in range(1, blocks):
                    sent = sent + picks[i][j] * wide[j * block : (j + 1) * block]
                outbox[which][g, i, column] = sent.astype(jnp.bfloat16)
            return carry

        lax.fori_loop(0, grouped[which], one_head, 0)
        each_halo(which, g, lambda copy: copy.start())

    position = lax.broadcasted_iota(jnp.int32, (block, HD), 0)
    spare = padded - blocks - len(slots)

    to_base_two = scale * math.log2(math.e)

    def listed_rows(which, h):
        pieces = [store[which, h]]
        for i in range(len(slots)):
            pieces.append(halo[which][lax.div(h, grouped[which]), i, lax.rem(h, grouped[which])])
        if spare > 0:
            pieces.append(jnp.zeros((spare * block, HD), jnp.bfloat16))
        return jnp.concatenate(pieces, axis=0)

    def softmax(scores):
        halves, denominators = [], []
        for b in range(blocks):
            of_block = scores[b * block : (b + 1) * block] + bias_ref[b : b + 1, :]
            peak = jnp.max(of_block, axis=1, keepdims=True)
            weights = jnp.exp2((of_block - peak) * to_base_two)
            denominators.append(jnp.sum(weights, axis=1, keepdims=True))
            halves.append(weights.astype(jnp.bfloat16))
        return jnp.concatenate(halves, axis=0), 1.0 / jnp.concatenate(denominators, axis=0)

    def turned_back(mixed):
        first = mixed.astype(jnp.bfloat16)
        rest = mixed - first.astype(jnp.float32)
        second = rest.astype(jnp.bfloat16)
        third = (rest - second.astype(jnp.float32)).astype(jnp.bfloat16)
        sign = sign_ref[...]
        turned = jnp.dot(
            jnp.concatenate([first, second], axis=1),
            jnp.concatenate([sign, sign], axis=0),
            preferred_element_type=jnp.float32,
        )
        return (turned + jnp.dot(third, sign, preferred_element_type=jnp.float32)) * scale

    def attend(g):
        columns = range(query_heads)
        queries = [rotated(2, g, column) for column in columns]
        scores = [
            lax.dot_general(
                queries[column],
                listed_rows(0, g * query_heads + column),
                (((1,), (1,)), ((), ())),
                preferred_element_type=jnp.float32,
            )
            for column in columns
        ]
        weighted = [softmax(of_head) for of_head in scores]
        mixed = [
            jnp.dot(
                weighted[column][0],
                listed_rows(1, g * query_heads + column),
                preferred_element_type=jnp.float32,
            )
            * weighted[column][1]
            for column in columns
        ]
        results = [turned_back(of_head) for of_head in mixed]
        for b in range(blocks):
            live = position < tokens_ref[me * blocks + b]
            for column in columns:
                result = jnp.where(live, results[column][b * block : (b + 1) * block], 0.0)
                for owner in range(count_head):
                    staged[g, owner, b, :, column * HD : (column + 1) * HD] = result[
                        owner * part : (owner + 1) * part
                    ].astype(jnp.bfloat16)

    pl.when(hub)(lambda: pl.semaphore_wait(column_side, count_tm - 1))
    pl.when(has_low)(lambda: pl.semaphore_wait(column_down, 1))
    pl.when(has_high)(lambda: tell(column_down, my_head + 1))
    for which, g in pairs_of:
        spread(which, g)

    def attend_group(g, carry):
        arrived(2, g)
        for which in range(2):
            for j in range(groups[which]):
                first = j * grouped[which] - g * query_heads
                pl.when((first >= 0) & (first < query_heads))(
                    lambda which=which, j=j: each_halo(
                        which, j, lambda copy: copy.wait_recv(), arriving=True
                    )
                )
        attend(g)
        for peer in far_first:
            pl.when(first_served(peer))(lambda peer=peer: back_copy(peer, g).start())
        back_own(g).start()
        pl.when(g >= DEFER)(lambda: send_later(g - DEFER))
        return carry

    def first_served(peer):
        return (my_head == 0) | (peer == 0)

    def send_later(g):
        for peer in far_first:
            later = jnp.logical_not(first_served(peer))
            pl.when(later)(lambda peer=peer: back_copy(peer, g).start())

    lax.fori_loop(0, query_groups, attend_group, 0)
    for g in range(max(0, query_groups - DEFER), query_groups):
        send_later(g)

    for which in range(3):
        for g in range(groups[which]):
            for peer in others:
                head_copy(which, peer, g).wait_send()
            if which < 2:
                each_halo(which, g, lambda copy: copy.wait_send())
    for g in range(query_groups):
        for peer in others:
            back_copy(peer, g).wait_send()
            back_copy(peer, g, source=peer).wait_recv()
        back_own(g).wait()


def shards(query_rows, key_rows, value_rows, pair_list, block_tokens):
    count_head = lax.axis_size("head")
    count_tm = lax.axis_size("tm")
    blocks, part, full_width = query_rows.shape
    block = part * count_head
    heads = full_width // (HD * count_head)
    total_blocks, listed = pair_list.shape
    slots = incoming_slots(count_tm)
    filled = blocks + len(slots)
    per_lane_tile = max(1, LANES // block)
    padded = -(-filled // per_lane_tile) * per_lane_tile
    shard_rows = -(-count_tm // 8) * 8
    key_heads = heads_together(heads, KEY_HEADS)
    value_heads = heads_together(heads, VALUE_HEADS)
    query_heads = heads_together(heads, QUERY_HEADS)
    grouped = (key_heads, value_heads, query_heads)
    key_groups, value_groups, query_groups = [heads // size for size in grouped]
    most = max(key_groups, value_groups, query_groups)
    sizes = (
        count_head, count_tm, blocks, part, heads, block, total_blocks, slots, padded, grouped
    )
    rounds = max(1, count_head - 2)
    in_hbm = pl.BlockSpec(memory_space=pltpu.HBM)
    dma = pltpu.SemaphoreType.DMA
    return pl.pallas_call(
        functools.partial(kernel, sizes),
        out_shape=jax.ShapeDtypeStruct(query_rows.shape, jnp.bfloat16),
        in_specs=[in_hbm] * 5,
        out_specs=in_hbm,
        scratch_shapes=[
            pltpu.VMEM((key_groups, count_head, blocks, part, key_heads * HD), jnp.bfloat16),
            pltpu.VMEM((value_groups, count_head, blocks, part, value_heads * HD), jnp.bfloat16),
            pltpu.VMEM((query_groups, count_head, blocks, part, query_heads * HD), jnp.bfloat16),
            pltpu.VMEM((2, heads, blocks * block, HD), jnp.bfloat16),
            pltpu.VMEM((key_groups, len(slots), key_heads, block, HD), jnp.bfloat16),
            pltpu.VMEM((value_groups, len(slots), value_heads, block, HD), jnp.bfloat16),
            pltpu.VMEM((key_groups, len(slots), key_heads, block, HD), jnp.bfloat16),
            pltpu.VMEM((value_groups, len(slots), value_heads, block, HD), jnp.bfloat16),
            pltpu.VMEM((query_groups, count_head, blocks, part, query_heads * HD), jnp.bfloat16),
            pltpu.VMEM((total_blocks, listed), jnp.int32),
            pltpu.SMEM((total_blocks,), jnp.int32),
            pltpu.VMEM((count_tm, blocks, LANES), jnp.float32),
            pltpu.VMEM((NEAR_CAP, count_tm, 1, LANES), jnp.float32),
            pltpu.VMEM((shard_rows, LANES), jnp.float32),
            pltpu.VMEM((blocks, padded * block), jnp.float32),
            pltpu.VMEM((HD, HD), jnp.bfloat16),
            dma((3, count_head, most)),
            dma((3, count_head, most)),
            dma((3, most)),
            pltpu.SemaphoreType.REGULAR((rounds,)),
            pltpu.SemaphoreType.REGULAR((rounds,)),
            pltpu.SemaphoreType.REGULAR,
            pltpu.SemaphoreType.REGULAR,
            pltpu.SemaphoreType.REGULAR,
            dma((2, most, count_tm - 1)),
            dma((2, most, count_tm - 1)),
            dma((count_head, query_groups)),
            dma((count_head, query_groups)),
            dma((query_groups,)),
            dma(()),
            dma(()),
        ],
        compiler_params=pltpu.CompilerParams(
            collective_id=0, has_side_effects=True, vmem_limit_bytes=32 * 1024 * 1024
        ),
    )(*[pltpu.with_memory_space_constraint(x, pltpu.HBM) for x in (query_rows, key_rows, value_rows, pair_list, block_tokens)])


def solution(mesh):
    placed = (
        P(("grp", "tm"), "head", None),
        P(("grp", "tm"), "head", None),
        P(("grp", "tm"), "head", None),
        P("grp", None),
        P("grp"),
    )
    return jax.shard_map(
        shards,
        mesh=mesh,
        in_specs=placed,
        out_specs=P(("grp", "tm"), "head", None),
        check_vma=False,
    )
```

time: 42.6 us -> 41.1 us (0.965)
  Pallas kernels: 41.7 us -> 40.2 us
    pallas_call x1, Pallas kernels: 41.7 us -> 40.2 us  [shards(): pl.pallas_call(functools.partial(kernel, sizes), out_shape=jax.ShapeDtype...]
where the time goes in v2:
time: 41.1 us; the launch traced here: 41 us
  Pallas kernels  40.2 us (98%)
  local copies, waits for them, and re-layouts  0.75 us (2%)
    pallas_call x1, Pallas kernels, shards(): pl.pallas_call(functools.partial(kernel, sizes), out_shape=jax.ShapeDtype...  40.2 us

profile of v2, /device:TPU:0, one launch (start us, length us, event | category | flops | bytes accessed | tf_op | source)
XLA Modules:
  0.0 41.0 jit_solution(15620277948226475092)
XLA Ops:
  0.0 40.2 %shard_map.55 = bf16[4,16,3072]{2,1,0:T(8,128)(2,1)S(1)} custom-call(bf16[4,16,3072]{2,1,0:T(8,128)(2,1)} %query_ref.1, bf16[4,16,3072]{2,1,0:T(8,128)(2,1)} %key_ref.1, bf16[4,16,3072]{2,1,0:T(8,128)(2,1)} %value_ref.1, s32[16,32]{1,0:T(8,128)} %pair_ref.1, s32[16]{0:T(128)} %tokens_far.1), custom_call_target="tpu_custom_call" | custom-call | tf_op jit(solution)/shard_map/pallas_call | solution.py:490
  40.2 0.7 %copy.7 = bf16[4,16,3072]{2,1,0:T(8,128)(2,1)} copy(bf16[4,16,3072]{2,1,0:T(8,128)(2,1)S(1)} %shard_map.55) | data formatting | bytes 786432

commit v3 on v2

--- a/solution.py
+++ b/solution.py
@@ -13,12 +13,9 @@
 FAR_CAP = 1
 LANES = 128
 EARLY = 2
-DEFER = 0
-PAIRS_BY_PEER = False
-QUERIES_BY_PEER = False
-KEY_HEADS = 3
-VALUE_HEADS = 3
-QUERY_HEADS = 3
+DEFER = 1
+PAIR_HEADS = 2
+QUERY_HEADS = 2
 MESH = pl.DeviceIdType.MESH
 
 
@@ -52,14 +49,12 @@
     pair_ref,
     tokens_far,
     out_ref,
-    key_in,
-    value_in,
+    packed,
+    pair_in,
     query_in,
     store,
-    key_outbox,
-    value_outbox,
-    key_halo,
-    value_halo,
+    outbox,
+    halo,
     staged,
     pair_here,
     tokens_ref,
@@ -70,7 +65,9 @@
     sign_ref,
     head_send,
     head_recv,
-    head_local,
+    pair_local,
+    query_local,
+    pack_sem,
     entered_low,
     entered_high,
     column_up,
@@ -85,10 +82,9 @@
     tokens_sem,
 ):
     count_head, count_tm, blocks, part, heads, block, total_blocks, slots, padded, grouped = sizes
-    sources, landed = (key_ref, value_ref, query_ref), (key_in, value_in, query_in)
-    outbox, halo = (key_outbox, value_outbox), (key_halo, value_halo)
-    groups = [heads // size for size in grouped]
-    query_heads, query_groups = grouped[2], groups[2]
+    pairs = (key_ref, value_ref)
+    pair_heads, query_heads = grouped
+    pair_groups, query_groups = heads // pair_heads, heads // query_heads
     offsets = range(1, count_tm)
     places = {o: [p for k, p in slots if k == o] for o in offsets}
     width = heads * HD
@@ -105,33 +101,53 @@
     def columns_of(owner, first, count):
         return pl.ds(pl.multiple_of(owner * width + first * HD, HD), count * HD)
 
-    def head_copy(which, peer, g, source=None):
+    def head_copy(is_query, peer, g, source=None):
         source = my_head if source is None else source
+        if is_query:
+            sent = query_ref.at[:, :, columns_of(peer, g * query_heads, query_heads)]
+            landing = query_in.at[g, source]
+        else:
+            sent, landing = packed.at[g, peer], pair_in.at[g, source]
         return pltpu.make_async_remote_copy(
-            src_ref=sources[which].at[:, :, columns_of(peer, g * grouped[which], grouped[which])],
-            dst_ref=landed[which].at[g, source],
-            send_sem=head_send.at[which, peer, g],
-            recv_sem=head_recv.at[which, source, g],
+            src_ref=sent,
+            dst_ref=landing,
+            send_sem=head_send.at[is_query, peer, g],
+            recv_sem=head_recv.at[is_query, source, g],
             device_id={"head": peer},
             device_id_type=MESH,
         )
 
-    def local_copy(which, g):
+    def pair_columns(which, owner, g):
+        return pairs[which].at[:, :, columns_of(owner, g * pair_heads, pair_heads)]
+
+    def pack_copy(which, peer, g):
         return pltpu.make_async_copy(
-            sources[which].at[:, :, columns_of(my_head, g * grouped[which], grouped[which])],
-            landed[which].at[g, my_head],
-            head_local.at[which, g],
-        )
-
-    def halo_copy(which, g, offset, count, arriving=False):
+            pair_columns(which, peer, g), packed.at[g, peer, which], pack_sem.at[which, peer, g]
+        )
+
+    def own_pair(which, g):
+        return pltpu.make_async_copy(
+            pair_columns(which, my_head, g),
+            pair_in.at[g, my_head, which],
+            pair_local.at[which, g],
+        )
+
+    def own_query(g):
+        return pltpu.make_async_copy(
+            query_ref.at[:, :, columns_of(my_head, g * query_heads, query_heads)],
+            query_in.at[g, my_head],
+            query_local.at[g],
+        )
+
+    def halo_copy(g, offset, count, arriving=False):
         peer = lax.rem(me + offset, count_tm)
         first = slot_of[(offset, 0)]
         landing = first if arriving else slot_of[(count_tm - offset, 0)]
         return pltpu.make_async_remote_copy(
-            src_ref=outbox[which].at[g, pl.ds(first, count)],
-            dst_ref=halo[which].at[g, pl.ds(landing, count)],
-            send_sem=halo_send.at[which, g, offset - 1],
-            recv_sem=halo_recv.at[which, g, (offset if arriving else count_tm - offset) - 1],
+            src_ref=outbox.at[g, pl.ds(first, count)],
+            dst_ref=halo.at[g, pl.ds(landing, count)],
+            send_sem=halo_send.at[g, offset - 1],
+            recv_sem=halo_recv.at[g, (offset if arriving else count_tm - offset) - 1],
             device_id={"tm": peer},
             device_id_type=MESH,
         )
@@ -140,16 +156,16 @@
         peer = lax.rem(me + offset, count_tm)
         return (peer == me + 1) | (peer == me - 1)
 
-    def each_halo(which, g, action, arriving=False):
+    def each_halo(g, action, arriving=False):
         for offset in offsets:
             full = len(places[offset])
             if full == FAR_CAP:
-                action(halo_copy(which, g, offset, full, arriving))
+                action(halo_copy(g, offset, full, arriving))
             else:
                 near = beside(offset)
-                pl.when(near)(lambda o=offset, n=full: action(halo_copy(which, g, o, n, arriving)))
+                pl.when(near)(lambda o=offset, n=full: action(halo_copy(g, o, n, arriving)))
                 pl.when(jnp.logical_not(near))(
-                    lambda o=offset: action(halo_copy(which, g, o, FAR_CAP, arriving))
+                    lambda o=offset: action(halo_copy(g, o, FAR_CAP, arriving))
                 )
 
     def back_copy(peer, g, source=None):
@@ -192,14 +208,17 @@
     pair_copy.start()
     tokens_copy = pltpu.make_async_copy(tokens_far, tokens_ref, tokens_sem)
     tokens_copy.start()
-    for which in range(3):
-        for g in range(groups[which]):
-            local_copy(which, g).start()
+    for g in range(pair_groups):
+        for peer in others:
+            for which in range(2):
+                pack_copy(which, peer, g).start()
+        for which in range(2):
+            own_pair(which, g).start()
+    for g in range(query_groups):
+        own_query(g).start()
 
     def clear(i):
-        for which in range(2):
-            shape = (groups[which], grouped[which], block, HD)
-            halo[which][:, i] = jnp.zeros(shape, jnp.bfloat16)
+        halo[:, i] = jnp.zeros((pair_groups, 2, pair_heads, block, HD), jnp.bfloat16)
 
     for i, (offset, place) in enumerate(slots):
         if place >= FAR_CAP:
@@ -210,19 +229,19 @@
     awaited = neighbours + jnp.where(hub, count_tm - 1, 0)
     pl.semaphore_wait(pltpu.get_barrier_semaphore(), awaited)
 
-    pairs_of = sorted(
-        ((which, g) for which in range(2) for g in range(groups[which])),
-        key=lambda piece: piece[1] * grouped[piece[0]],
-    )
-    queries_of = [(2, g) for g in range(query_groups)]
-    early = pairs_of[:EARLY]
+    pieces = [(0, g) for g in range(pair_groups)] + [(1, g) for g in range(query_groups)]
+    early = pieces[: min(EARLY, pair_groups)]
+    for _, g in early:
+        for peer in others:
+            for which in range(2):
+                pack_copy(which, peer, g).wait()
 
     def start_at(distance):
         for side in (-distance, distance):
             peer = my_head + side
             inside = (peer >= 0) & (peer < count_head)
-            for which, g in early:
-                pl.when(inside)(lambda p=peer, w=which, g=g: head_copy(w, p, g).start())
+            for kind, g in early:
+                pl.when(inside)(lambda p=peer, k=kind, g=g: head_copy(k, p, g).start())
 
     for distance in range(1, count_head):
         if distance > 1:
@@ -238,14 +257,13 @@
     pl.when(my_head < count_head - 1)(lambda: pl.semaphore_wait(column_up, 1))
     pl.when(has_low)(lambda: tell(column_up, my_head - 1))
 
-    for pieces, by_peer in ((pairs_of, PAIRS_BY_PEER), (queries_of, QUERIES_BY_PEER)):
-        if by_peer:
-            plan = [(piece, peer) for peer in far_first for piece in pieces]
-        else:
-            plan = [(piece, peer) for piece in pieces for peer in far_first]
-        for (which, g), peer in plan:
-            if (which, g) not in early:
-                head_copy(which, peer, g).start()
+    for kind, g in pieces:
+        if (kind, g) not in early:
+            for peer in far_first:
+                if kind == 0:
+                    for which in range(2):
+                        pack_copy(which, peer, g).wait()
+                head_copy(kind, peer, g).start()
 
     @pl.when(hub)
     def _():
@@ -259,12 +277,12 @@
 
     pair_copy.wait()
     tokens_copy.wait()
-    pairs = pair_here[...]
+    listing = pair_here[...]
     lane = lax.broadcasted_iota(jnp.int32, (1, LANES), 1)
     listed = jnp.zeros((total_blocks, LANES), jnp.float32)
     token_row = jnp.zeros((1, LANES), jnp.float32)
     for k in range(total_blocks):
-        found = jnp.max(jnp.where(pairs == k, 1.0, 0.0), axis=1, keepdims=True)
+        found = jnp.max(jnp.where(listing == k, 1.0, 0.0), axis=1, keepdims=True)
         here = jnp.where(lane == k, 1.0, 0.0)
         listed = listed + found * here
         token_row = token_row + here * tokens_ref[k].astype(jnp.float32)
@@ -313,39 +331,39 @@
         key_end = key_end + inside * (kept + float(i * block))
     bias_ref[...] = jnp.where(key_lane.astype(jnp.float32) < key_end, 0.0, -1e30)
 
-    def arrived(which, g):
-        local_copy(which, g).wait()
+    def arrived(kind, g):
         for peer in others:
-            head_copy(which, peer, g, source=peer).wait_recv()
-
-    def rotated(which, g, column):
+            head_copy(kind, peer, g, source=peer).wait_recv()
+
+    def rotated(landed, column):
         lanes = pl.ds(pl.multiple_of(column * HD, HD), HD)
         rows = jnp.concatenate(
-            [
-                landed[which][g, :, b, :, lanes].astype(jnp.float32).reshape(block, HD)
-                for b in range(blocks)
-            ],
+            [landed[:, b, :, lanes].astype(jnp.float32).reshape(block, HD) for b in range(blocks)],
             axis=0,
         ).astype(jnp.bfloat16)
         turned = jnp.dot(rows, sign_ref[...], preferred_element_type=jnp.float32) * scale
         return turned.astype(jnp.bfloat16)
 
-    def spread(which, g):
-        arrived(which, g)
+    def spread(g, carry):
+        for which in range(2):
+            own_pair(which, g).wait()
+        arrived(0, g)
 
         def one_head(column, carry):
-            turned = rotated(which, g, column)
-            store[which, g * grouped[which] + column] = turned
-            wide = turned.astype(jnp.float32)
-            for i in range(len(slots)):
-                sent = picks[i][0] * wide[0:block]
-                for j in range(1, blocks):
-                    sent = sent + picks[i][j] * wide[j * block : (j + 1) * block]
-                outbox[which][g, i, column] = sent.astype(jnp.bfloat16)
+            for which in range(2):
+                turned = rotated(pair_in.at[g, :, which], column)
+                store[which, g * pair_heads + column] = turned
+                wide = turned.astype(jnp.float32)
+                for i in range(len(slots)):
+                    sent = picks[i][0] * wide[0:block]
+                    for j in range(1, blocks):
+                        sent = sent + picks[i][j] * wide[j * block : (j + 1) * block]
+                    outbox[g, i, which, column] = sent.astype(jnp.bfloat16)
             return carry
 
-        lax.fori_loop(0, grouped[which], one_head, 0)
-        each_halo(which, g, lambda copy: copy.start())
+        lax.fori_loop(0, pair_heads, one_head, 0)
+        each_halo(g, lambda copy: copy.start())
+        return carry
 
     position = lax.broadcasted_iota(jnp.int32, (block, HD), 0)
     spare = padded - blocks - len(slots)
@@ -355,7 +373,7 @@
     def listed_rows(which, h):
         pieces = [store[which, h]]
         for i in range(len(slots)):
-            pieces.append(halo[which][lax.div(h, grouped[which]), i, lax.rem(h, grouped[which])])
+            pieces.append(halo[lax.div(h, pair_heads), i, which, lax.rem(h, pair_heads)])
         if spare > 0:
             pieces.append(jnp.zeros((spare * block, HD), jnp.bfloat16))
         return jnp.concatenate(pieces, axis=0)
@@ -385,7 +403,7 @@
 
     def attend(g):
         columns = range(query_heads)
-        queries = [rotated(2, g, column) for column in columns]
+        queries = [rotated(query_in.at[g], column) for column in columns]
         scores = [
             lax.dot_general(
                 queries[column],
@@ -418,44 +436,40 @@
     pl.when(hub)(lambda: pl.semaphore_wait(column_side, count_tm - 1))
     pl.when(has_low)(lambda: pl.semaphore_wait(column_down, 1))
     pl.when(has_high)(lambda: tell(column_down, my_head + 1))
-    for which, g in pairs_of:
-        spread(which, g)
+    lax.fori_loop(0, pair_groups, spread, 0)
 
     def attend_group(g, carry):
-        arrived(2, g)
-        for which in range(2):
-            for j in range(groups[which]):
-                first = j * grouped[which] - g * query_heads
-                pl.when((first >= 0) & (first < query_heads))(
-                    lambda which=which, j=j: each_halo(
-                        which, j, lambda copy: copy.wait_recv(), arriving=True
-                    )
-                )
+        own_query(g).wait()
+        arrived(1, g)
+        for j in range(pair_groups):
+            first = j * pair_heads - g * query_heads
+            pl.when((first >= 0) & (first < query_heads))(
+                lambda j=j: each_halo(j, lambda copy: copy.wait_recv(), arriving=True)
+            )
         attend(g)
         for peer in far_first:
-            pl.when(first_served(peer))(lambda peer=peer: back_copy(peer, g).start())
+            now = jnp.logical_not(deferred(peer))
+            pl.when(now)(lambda peer=peer: back_copy(peer, g).start())
         back_own(g).start()
-        pl.when(g >= DEFER)(lambda: send_later(g - DEFER))
+        pl.when(g >= DEFER)(lambda: send_deferred(g - DEFER))
         return carry
 
-    def first_served(peer):
-        return (my_head == 0) | (peer == 0)
-
-    def send_later(g):
+    def deferred(peer):
+        return (my_head > 0) & (peer > 0)
+
+    def send_deferred(g):
         for peer in far_first:
-            later = jnp.logical_not(first_served(peer))
-            pl.when(later)(lambda peer=peer: back_copy(peer, g).start())
+            pl.when(deferred(peer))(lambda peer=peer: back_copy(peer, g).start())
 
     lax.fori_loop(0, query_groups, attend_group, 0)
     for g in range(max(0, query_groups - DEFER), query_groups):
-        send_later(g)
-
-    for which in range(3):
-        for g in range(groups[which]):
-            for peer in others:
-                head_copy(which, peer, g).wait_send()
-            if which < 2:
-                each_halo(which, g, lambda copy: copy.wait_send())
+        send_deferred(g)
+
+    for kind, g in pieces:
+        for peer in others:
+            head_copy(kind, peer, g).wait_send()
+        if kind == 0:
+            each_halo(g, lambda copy: copy.wait_send())
     for g in range(query_groups):
         for peer in others:
             back_copy(peer, g).wait_send()
@@ -475,12 +489,14 @@
     per_lane_tile = max(1, LANES // block)
     padded = -(-filled // per_lane_tile) * per_lane_tile
     shard_rows = -(-count_tm // 8) * 8
-    key_heads = heads_together(heads, KEY_HEADS)
-    value_heads = heads_together(heads, VALUE_HEADS)
+    pair_heads = heads_together(heads, PAIR_HEADS)
     query_heads = heads_together(heads, QUERY_HEADS)
-    grouped = (key_heads, value_heads, query_heads)
-    key_groups, value_groups, query_groups = [heads // size for size in grouped]
-    most = max(key_groups, value_groups, query_groups)
+    grouped = (pair_heads, query_heads)
+    pair_groups, query_groups = [heads // size for size in grouped]
+    most = max(pair_groups, query_groups)
+    pair_shape = (pair_groups, count_head, 2, blocks, part, pair_heads * HD)
+    query_shape = (query_groups, count_head, blocks, part, query_heads * HD)
+    halo_shape = (pair_groups, len(slots), 2, pair_heads, block, HD)
     sizes = (
         count_head, count_tm, blocks, part, heads, block, total_blocks, slots, padded, grouped
     )
@@ -493,15 +509,13 @@
         in_specs=[in_hbm] * 5,
         out_specs=in_hbm,
         scratch_shapes=[
-            pltpu.VMEM((key_groups, count_head, blocks, part, key_heads * HD), jnp.bfloat16),
-            pltpu.VMEM((value_groups, count_head, blocks, part, value_heads * HD), jnp.bfloat16),
-            pltpu.VMEM((query_groups, count_head, blocks, part, query_heads * HD), jnp.bfloat16),
+            pltpu.VMEM(pair_shape, jnp.bfloat16),
+            pltpu.VMEM(pair_shape, jnp.bfloat16),
+            pltpu.VMEM(query_shape, jnp.bfloat16),
             pltpu.VMEM((2, heads, blocks * block, HD), jnp.bfloat16),
-            pltpu.VMEM((key_groups, len(slots), key_heads, block, HD), jnp.bfloat16),
-            pltpu.VMEM((value_groups, len(slots), value_heads, block, HD), jnp.bfloat16),
-            pltpu.VMEM((key_groups, len(slots), key_heads, block, HD), jnp.bfloat16),
-            pltpu.VMEM((value_groups, len(slots), value_heads, block, HD), jnp.bfloat16),
-            pltpu.VMEM((query_groups, count_head, blocks, part, query_heads * HD), jnp.bfloat16),
+            pltpu.VMEM(halo_shape, jnp.bfloat16),
+            pltpu.VMEM(halo_shape, jnp.bfloat16),
+            pltpu.VMEM(query_shape, jnp.bfloat16),
             pltpu.VMEM((total_blocks, listed), jnp.int32),
             pltpu.SMEM((total_blocks,), jnp.int32),
             pltpu.VMEM((count_tm, blocks, LANES), jnp.float32),
@@ -509,16 +523,18 @@
             pltpu.VMEM((shard_rows, LANES), jnp.float32),
             pltpu.VMEM((blocks, padded * block), jnp.float32),
             pltpu.VMEM((HD, HD), jnp.bfloat16),
-            dma((3, count_head, most)),
-            dma((3, count_head, most)),
-            dma((3, most)),
+            dma((2, count_head, most)),
+            dma((2, count_head, most)),
+            dma((2, pair_groups)),
+            dma((query_groups,)),
+            dma((2, count_head, pair_groups)),
             pltpu.SemaphoreType.REGULAR((rounds,)),
             pltpu.SemaphoreType.REGULAR((rounds,)),
             pltpu.SemaphoreType.REGULAR,
             pltpu.SemaphoreType.REGULAR,
             pltpu.SemaphoreType.REGULAR,
-            dma((2, most, count_tm - 1)),
-            dma((2, most, count_tm - 1)),
+            dma((pair_groups, count_tm - 1)),
+            dma((pair_groups, count_tm - 1)),
             dma((count_head, query_groups)),
             dma((count_head, query_groups)),
             dma((query_groups,)),

time: 41.1 us -> 40.5 us (0.985)
  Pallas kernels: 40.2 us -> 39.6 us
    pallas_call x1, Pallas kernels: 40.2 us -> 39.6 us  [shards(): pl.pallas_call(functools.partial(kernel, sizes), out_shape=jax.ShapeDtype...]
where the time goes in v3:
time: 40.5 us; the launch traced here: 40.3 us
  Pallas kernels  39.6 us (98%)
  local copies, waits for them, and re-layouts  0.75 us (2%)
    pallas_call x1, Pallas kernels, shards(): pl.pallas_call(functools.partial(kernel, sizes), out_shape=jax.ShapeDtype...  39.6 us

profile of v3, /device:TPU:0, one launch (start us, length us, event | category | flops | bytes accessed | tf_op | source)
XLA Modules:
  0.0 40.3 jit_solution(3156130384460923136)
XLA Ops:
  0.0 39.6 %shard_map.55 = bf16[4,16,3072]{2,1,0:T(8,128)(2,1)S(1)} custom-call(bf16[4,16,3072]{2,1,0:T(8,128)(2,1)} %query_ref.1, bf16[4,16,3072]{2,1,0:T(8,128)(2,1)} %key_ref.1, bf16[4,16,3072]{2,1,0:T(8,128)(2,1)} %value_ref.1, s32[16,32]{1,0:T(8,128)} %pair_ref.1, s32[16]{0:T(128)} %tokens_far.1), custom_call_target="tpu_custom_call" | custom-call | tf_op jit(solution)/shard_map/pallas_call | solution.py:506
  39.6 0.7 %copy.7 = bf16[4,16,3072]{2,1,0:T(8,128)(2,1)} copy(bf16[4,16,3072]{2,1,0:T(8,128)(2,1)S(1)} %shard_map.55) | data formatting | bytes 786432
